TPU v7x, 32 devices: a whole 2x2x4 slice. The times are simulated.
32 devices in a mesh: dp: 2 (over core), ctx: 4 (over y, x), tp: 4 (over z).
Axes of the slice: x: 2, y: 2, z: 4, core: 2. Of those that a mesh axis runs over, the one named last changes fastest.
Arguments:
- hidden_in: bfloat16 [2, 1024, 768], P('dp', 'ctx'), may hold values from -6 to 6
- span_order: int32 [2, 8], P('dp'), may hold values from 0 to 7, each once within a row
- norm_gains: float32 [2, 768], replicated, may hold values from 0.5 to 1.5
- norm_biases: float32 [2, 768], replicated, may hold values from -1.75 to 1.75
- w_qkv: bfloat16 [768, 2304], P(('dp', 'ctx'), 'tp')
- qv_bias: float32 [1536], P('tp'), may hold values from -3 to 3
- w_dense: bfloat16 [768, 768], P(('dp', 'ctx'), 'tp'), may hold values from -0.875 to 0.875
- w_up: bfloat16 [768, 3072], P(('dp', 'ctx'), 'tp'), may hold values from -0.21875 to 0.21875
- up_bias: float32 [3072], P('tp'), may hold values from -3 to 3
- w_down: bfloat16 [768, 3072], P(('dp', 'ctx'), 'tp'), may hold values from -0.109375 to 0.109375
- out_bias: float32 [768], replicated, may hold values from -3 to 3
- grad_out: bfloat16 [2, 1024, 768], P('dp', 'ctx'), may hold values from -6 to 6
Outputs:
- layer_out: bfloat16 [2, 1024, 768], P('dp', 'ctx')
- grad_in: bfloat16 [2, 1024, 768], P('dp', 'ctx')
- grad_norm_gains: float32 [2, 768], replicated
- grad_norm_biases: float32 [2, 768], replicated
- grad_qkv: float32 [768, 2304], P(('dp', 'ctx'), 'tp')
- grad_qv_bias: float32 [1536], P('tp')
- grad_dense: float32 [768, 768], P(('dp', 'ctx'), 'tp')
- grad_up: float32 [768, 3072], P(('dp', 'ctx'), 'tp')
- grad_up_bias: float32 [3072], P('tp')
- grad_down: float32 [768, 3072], P(('dp', 'ctx'), 'tp')
- grad_out_bias: float32 [768], replicated
Inputs may be any that keep to these rules, and one draw needn't show every extreme that they name: `span_order`: each row lists every block index once.
All inputs are finite; a program needn't handle non-finite values.
Results may differ from a plain program's by a relative error of at most 0.0084.
Values may be sent and summed in bfloat16 or wider, within the bound.
A program may use at most 128 MiB of HBM per device.

v0:
```python
import math

import jax
import jax.numpy as jnp
from jax import lax
from jax.sharding import PartitionSpec as P

HD = 64
ROT = 16
SPAN = 128


EPS = 1e-05
NEG = -1e30


def layer_norm(values, gain_vec, shift_vec):
    row_mean = jnp.mean(values, axis=-1, keepdims=True)
    centered = values - row_mean
    variance = jnp.mean(centered * centered, axis=-1, keepdims=True)
    inv_std = lax.rsqrt(variance + EPS)
    normed = centered * inv_std
    return (normed * gain_vec + shift_vec, normed, inv_std)


def norm_back(grad_normed, normed, inv_std, gain_vec):
    scaled = grad_normed * gain_vec
    return inv_std * (
        scaled
        - jnp.mean(scaled, axis=-1, keepdims=True)
        - normed * jnp.mean(scaled * normed, axis=-1, keepdims=True)
    )


def rotary_tables(positions, rot_dims):
    half_rot = rot_dims // 2
    frequency = 1.0 / 10000.0 ** (jnp.arange(half_rot, dtype=jnp.float32) * (2.0 / rot_dims))
    angles = positions.astype(jnp.float32)[:, None] * frequency[None, :]
    return (jnp.cos(angles), jnp.sin(angles))


def rotate(vectors, cos_table, sin_table, rot_dims):
    half_rot = rot_dims // 2
    front_half = vectors[..., :half_rot]
    back_half = vectors[..., half_rot:rot_dims]
    cos_row = cos_table[:, None, :]
    sin_row = sin_table[:, None, :]
    return jnp.concatenate(
        [
            front_half * cos_row - back_half * sin_row,
            back_half * cos_row + front_half * sin_row,
            vectors[..., rot_dims:],
        ],
        axis=-1,
    )


def gelu_value(hidden):
    return 0.5 * hidden * (1.0 + jax.scipy.special.erf(hidden * (1.0 / math.sqrt(2.0))))


def gelu_slope(hidden):
    return 0.5 * (1.0 + jax.scipy.special.erf(hidden * (1.0 / math.sqrt(2.0)))) + hidden * jnp.exp(
        -0.5 * hidden * hidden
    ) * (1.0 / math.sqrt(2.0 * math.pi))


def on_device(
    hidden_in,
    span_order,
    norm_gains,
    norm_biases,
    w_qkv,
    qv_bias,
    w_dense,
    w_up,
    up_bias,
    w_down,
    out_bias,
    grad_out,
):
    tok_rows = hidden_in.shape[1]
    local_heads = qv_bias.shape[0] // (2 * HD)
    head_cols = local_heads * HD
    score_scale = 1.0 / math.sqrt(HD)
    positions = (
        span_order[0][:, None] * SPAN + jnp.arange(SPAN, dtype=jnp.int32)[None, :]
    ).reshape(-1)
    own_pos = lax.dynamic_slice_in_dim(positions, lax.axis_index("ctx") * tok_rows, tok_rows)
    full_qkv, full_dense, full_up, full_down = (
        lax.all_gather(w_qkv, ("dp", "ctx"), axis=0, tiled=True),
        lax.all_gather(w_dense, ("dp", "ctx"), axis=0, tiled=True),
        lax.all_gather(w_up, ("dp", "ctx"), axis=0, tiled=True),
        lax.all_gather(w_down, ("dp", "ctx"), axis=0, tiled=True),
    )
    inputs = hidden_in[0].astype(jnp.float32)
    normed_one, hat_one, inv_one = layer_norm(inputs, norm_gains[0], norm_biases[0])
    normed_two, hat_two, inv_two = layer_norm(inputs, norm_gains[1], norm_biases[1])
    attn_in = normed_one.astype(jnp.bfloat16)
    mlp_in = normed_two.astype(jnp.bfloat16)
    projected = jnp.dot(attn_in, full_qkv, preferred_element_type=jnp.float32).reshape(
        tok_rows, local_heads, 3, HD
    )
    bias_pair = qv_bias.reshape(local_heads, 2, HD)
    cos_table, sin_table = rotary_tables(own_pos, ROT)
    queries = rotate(projected[:, :, 0] + bias_pair[:, 0], cos_table, sin_table, ROT).astype(
        jnp.bfloat16
    )
    keys_rot = rotate(projected[:, :, 1], cos_table, sin_table, ROT).astype(jnp.bfloat16)
    values_in = (projected[:, :, 2] + bias_pair[:, 1]).astype(jnp.bfloat16)
    kv_flat = jnp.concatenate(
        [keys_rot.reshape(tok_rows, head_cols), values_in.reshape(tok_rows, head_cols)], axis=-1
    )

    def split_keys(kv_piece):
        piece_rows = kv_piece.shape[0]
        group_rows = math.gcd(piece_rows, 4 * tok_rows)
        block_count = piece_rows // group_rows
        key_pos = positions.reshape(block_count, group_rows)
        key_blocks = kv_piece[:, :head_cols].reshape(block_count, group_rows, local_heads, HD)
        value_blocks = kv_piece[:, head_cols:].reshape(block_count, group_rows, local_heads, HD)
        return (key_blocks, value_blocks, key_pos)

    def key_block(state_in, block_in):
        key_blk, value_blk, key_pos = block_in
        run_max, run_total, run_acc = state_in
        scores = (
            jnp.einsum("qhd,khd->hqk", queries, key_blk, preferred_element_type=jnp.float32)
            * score_scale
        )
        allowed = (key_pos[None, :] <= own_pos[:, None])[None]
        scores = jnp.where(allowed, scores, NEG)
        new_max = jnp.maximum(run_max, jnp.max(scores, axis=-1))
        weights = jnp.where(allowed, jnp.exp(scores - new_max[..., None]), 0.0)
        factor = jnp.exp(run_max - new_max)
        run_total = run_total * factor + jnp.sum(weights, axis=-1)
        run_acc = run_acc * factor[..., None] + jnp.einsum(
            "hqk,khd->hqd",
            weights.astype(jnp.bfloat16),
            value_blk,
            preferred_element_type=jnp.float32,
        )
        return ((new_max, run_total, run_acc), None)

    start_state = (
        jnp.full((local_heads, tok_rows), NEG, jnp.float32),
        jnp.zeros((local_heads, tok_rows), jnp.float32),
        jnp.zeros((local_heads, tok_rows, HD), jnp.float32),
    )
    state_out, unused = lax.scan(
        key_block, start_state, split_keys(lax.all_gather(kv_flat, "ctx", axis=0, tiled=True))
    )
    run_max, run_total, run_acc = state_out
    attn_out = (
        jnp.transpose(run_acc / run_total[..., None], (1, 0, 2))
        .reshape(tok_rows, head_cols)
        .astype(jnp.bfloat16)
    )
    log_total = run_max + jnp.log(run_total)
    attn_part = jnp.einsum("tc,dc->td", attn_out, full_dense, preferred_element_type=jnp.float32)
    hidden_pre = jnp.dot(mlp_in, full_up, preferred_element_type=jnp.float32) + up_bias
    activated = gelu_value(hidden_pre).astype(jnp.bfloat16)
    mlp_part = jnp.einsum("tf,df->td", activated, full_down, preferred_element_type=jnp.float32)
    branches = lax.psum(attn_part + mlp_part, "tp")
    layer_out = (inputs + out_bias + branches).astype(jnp.bfloat16)
    cotangent = grad_out[0]
    cot_float = cotangent.astype(jnp.float32)
    out_bias_grad = jnp.sum(cot_float, axis=0)
    down_grad = jnp.einsum("td,tf->df", cotangent, activated, preferred_element_type=jnp.float32)
    pre_grad = jnp.dot(cotangent, full_down, preferred_element_type=jnp.float32) * gelu_slope(
        hidden_pre
    )
    up_bias_grad = jnp.sum(pre_grad, axis=0)
    pre_grad_b = pre_grad.astype(jnp.bfloat16)
    up_grad = jnp.einsum("td,tf->df", mlp_in, pre_grad_b, preferred_element_type=jnp.float32)
    normed_two_grad = jnp.einsum(
        "tf,df->td", pre_grad_b, full_up, preferred_element_type=jnp.float32
    )
    dense_grad = jnp.einsum("td,tc->dc", cotangent, attn_out, preferred_element_type=jnp.float32)
    out_grad = (
        jnp.dot(cotangent, full_dense, preferred_element_type=jnp.float32)
        .astype(jnp.bfloat16)
        .reshape(tok_rows, local_heads, HD)
    )
    row_delta = jnp.sum(
        out_grad.astype(jnp.float32)
        * attn_out.reshape(tok_rows, local_heads, HD).astype(jnp.float32),
        axis=-1,
    ).T
    back_kv = lax.all_gather(kv_flat, "ctx", axis=0, tiled=True)

    def pair_grads(key_blk, value_blk, key_pos):
        scores = (
            jnp.einsum("qhd,khd->hqk", queries, key_blk, preferred_element_type=jnp.float32)
            * score_scale
        )
        allowed = (key_pos[None, :] <= own_pos[:, None])[None]
        prob_table = jnp.where(
            allowed, jnp.exp(jnp.where(allowed, scores, NEG) - log_total[..., None]), 0.0
        )
        prob_grad = jnp.einsum(
            "qhd,khd->hqk", out_grad, value_blk, preferred_element_type=jnp.float32
        )
        score_grad = (prob_table * (prob_grad - row_delta[..., None])).astype(jnp.bfloat16)
        return (prob_table, score_grad)

    def grad_block(query_acc, block_in):
        key_blk, value_blk, key_pos = block_in
        prob_table, score_grad = pair_grads(key_blk, value_blk, key_pos)
        query_acc = (
            query_acc
            + jnp.einsum("hqk,khd->hqd", score_grad, key_blk, preferred_element_type=jnp.float32)
            * score_scale
        )
        key_part = (
            jnp.einsum("hqk,qhd->khd", score_grad, queries, preferred_element_type=jnp.float32)
            * score_scale
        )
        value_part = jnp.einsum(
            "hqk,qhd->khd",
            prob_table.astype(jnp.bfloat16),
            out_grad,
            preferred_element_type=jnp.float32,
        )
        group_rows = key_blk.shape[0]
        return (
            query_acc,
            jnp.concatenate(
                [
                    key_part.reshape(group_rows, head_cols),
                    value_part.reshape(group_rows, head_cols),
                ],
                axis=-1,
            ),
        )

    query_acc, kv_terms = lax.scan(
        grad_block, jnp.zeros((local_heads, tok_rows, HD), jnp.float32), split_keys(back_kv)
    )
    kv_grads = lax.psum_scatter(
        kv_terms.reshape(back_kv.shape[0], 2 * head_cols), "ctx", scatter_dimension=0, tiled=True
    )
    key_grad = kv_grads[:, :head_cols].reshape(tok_rows, local_heads, HD)
    value_grad = kv_grads[:, head_cols:].reshape(tok_rows, local_heads, HD)
    query_pre = rotate(jnp.transpose(query_acc, (1, 0, 2)), cos_table, -sin_table, ROT)
    key_pre = rotate(key_grad, cos_table, -sin_table, ROT)
    qv_grad = jnp.stack([jnp.sum(query_pre, axis=0), jnp.sum(value_grad, axis=0)], axis=1).reshape(
        -1
    )
    proj_grad = (
        jnp.stack([query_pre, key_pre, value_grad], axis=2)
        .reshape(tok_rows, 3 * head_cols)
        .astype(jnp.bfloat16)
    )
    qkv_grad = jnp.einsum("td,tc->dc", attn_in, proj_grad, preferred_element_type=jnp.float32)
    normed_one_grad = jnp.einsum(
        "tc,dc->td", proj_grad, full_qkv, preferred_element_type=jnp.float32
    )
    full_one, full_two = lax.psum((normed_one_grad, normed_two_grad), "tp")
    gain_part = jnp.stack(
        [jnp.sum(full_one * hat_one, axis=0), jnp.sum(full_two * hat_two, axis=0)]
    )
    bias_part = jnp.stack([jnp.sum(full_one, axis=0), jnp.sum(full_two, axis=0)])
    input_grad = (
        cot_float
        + norm_back(full_one, hat_one, inv_one, norm_gains[0])
        + norm_back(full_two, hat_two, inv_two, norm_gains[1])
    ).astype(jnp.bfloat16)
    gains_total, biases_total, qv_total, up_bias_total, out_bias_total = lax.psum(
        (gain_part, bias_part, qv_grad, up_bias_grad, out_bias_grad), ("dp", "ctx")
    )
    qkv_total, dense_total, up_total, down_total = (
        lax.psum_scatter(qkv_grad, ("dp", "ctx"), scatter_dimension=0, tiled=True),
        lax.psum_scatter(dense_grad, ("dp", "ctx"), scatter_dimension=0, tiled=True),
        lax.psum_scatter(up_grad, ("dp", "ctx"), scatter_dimension=0, tiled=True),
        lax.psum_scatter(down_grad, ("dp", "ctx"), scatter_dimension=0, tiled=True),
    )
    return (
        layer_out[None],
        input_grad[None],
        gains_total,
        biases_total,
        qkv_total,
        qv_total,
        dense_total,
        up_total,
        up_bias_total,
        down_total,
        out_bias_total,
    )


def solution(mesh):
    placed = (
        P("dp", "ctx", None),
        P("dp", None),
        P(),
        P(),
        P(("dp", "ctx"), "tp"),
        P("tp"),
        P(("dp", "ctx"), "tp"),
        P(("dp", "ctx"), "tp"),
        P("tp"),
        P(("dp", "ctx"), "tp"),
        P(),
        P("dp", "ctx", None),
    )
    return jax.shard_map(
        on_device,
        mesh=mesh,
        in_specs=placed,
        out_specs=(
            P("dp", "ctx", None),
            P("dp", "ctx", None),
            P(),
            P(),
            P(("dp", "ctx"), "tp"),
            P("tp"),
            P(("dp", "ctx"), "tp"),
            P(("dp", "ctx"), "tp"),
            P("tp"),
            P(("dp", "ctx"), "tp"),
            P(),
        ),
        check_vma=False,
    )
```

profile of v0, /device:TPU:0, one launch (start us, length us, event | category | flops | bytes accessed | tf_op | source)
XLA Modules:
  0.0 318.5 jit_solution(16914696624962062334)
XLA Ops:
  8.1 0.7 all-gather.3.cloned.1.call-update
  8.8 0.7 all-gather.5.cloned.1.call-update
  9.6 1.1 convert_reduce_fusion
  10.7 1.2 fusion.49
  12.0 32.6 %all_gather.16 = bf16[768,576]{1,0:T(8,128)(2,1)S(1)} all-gather(bf16[96,576]{1,0:T(8,128)(2,1)} %param.16), channel_id=1, replica_groups=mesh['dp'=2,'ctx'=4,'tp'=4] {'dp','ctx'}, dimensions={0}, use_global_device_ids=true | all-gather | bytes 995328 | tf_op jit(solution)/shard_map/all_gather | solution.py:91
  44.6 0.6 copy.33
  45.2 0.6 slice_reduce_fusion
  45.9 0.6 fusion.61
  46.6 0.1 fusion.70
  47.0 0.1 fusion.79
  47.1 0.1 fusion.71
  47.3 20.8 %all_gather.17 = bf16[1024,384]{0,1:T(8,128)(2,1)S(1)} all-gather(bf16[256,384]{0,1:T(8,128)(2,1)S(1)} %pad_maximum_fusion.1), channel_id=1, replica_groups=mesh['dp'=2,'ctx'=4,'tp'=4] {'ctx'}, dimensions={0}, use_global_device_ids=true | all-gather | bytes 983040 | tf_op jit(solution)/shard_map/all_gather | solution.py:151
  68.1 0.2 broadcast_compare_fusion
  68.3 0.8 fusion.91
  69.2 1.0 fusion
  70.2 24.9 %all_gather.18 = bf16[768,192]{1,0:T(8,128)(2,1)S(1)} all-gather(bf16[96,192]{1,0:T(8,128)(2,1)S(1)} %copy-done.17), channel_id=1, replica_groups=mesh['dp'=2,'ctx'=4,'tp'=4] {'dp','ctx'}, dimensions={0}, use_global_device_ids=true | all-gather | bytes 331776 | tf_op jit(solution)/shard_map/all_gather | solution.py:92
  95.1 0.3 convolution_convert_fusion
  95.4 0.9 multiply_reduce_fusion.2
  96.3 1.2 multiply_convert_fusion
  97.5 0.4 convolution_multiply_fusion.1
  97.9 0.8 fusion.3
  98.7 1.3 pad_maximum_fusion
  100.1 2.0 fusion.13
  102.2 1.2 fusion.93
  103.5 1.8 convolution_add_fusion.1
  105.4 2.3 fusion.92
  107.6 1.4 fusion.74
  109.0 1.4 convolution_add_fusion
  110.4 20.8 %reduce-scatter.10.cloned.1.call-done = f32[256,384]{0,1:T(8,128)} async-done(((f32[1024,384]{0,1:T(8,128)}), f32[256,384]{0,1:T(8,128)}) %reduce-scatter.10.cloned.1.call-update) | async-done | bytes 393232 | tf_op jit(solution)/shard_map/reduce_scatter | solution.py:240
  131.2 1.1 slice_reduce_fusion.5
  132.4 0.9 slice.126
  133.5 1.4 fusion.94
  135.0 0.2 convolution_bitcast_fusion.1
  135.2 1.1 copy.40
  136.5 2.1 fusion.72
  138.6 0.2 reduce-scatter.18.cloned.1.call-start
  138.8 1.7 convolution_bitcast_fusion
  140.5 1.9 copy.42
  142.5 0.6 copy-done.14
  143.2 2.0 fusion.67
  145.2 0.1 fusion.76
  145.4 0.1 reshape.311
  145.4 84.1 %all-reduce.4.cloned.1.call-done = (f32[256,768]{1,0:T(8,128)}, f32[256,768]{1,0:T(8,128)}, f32[256,768]{1,0:T(8,128)}) async-done(((f32[256,768]{1,0:T(8,128)}, f32[256,768]{1,0:T(8,128)}, f32[256,768]{1,0:T(8,128)}), (f32[256,768]{1,0:T(8,128)}, f32[256,768]{1,0:T(8,128)}, f32[256,768]{1,0:T(8,128)})) %all-reduce.4.cloned.1.call-update) | async-done | bytes 2359312 | tf_op jit(solution)/shard_map/psum | solution.py:164
  229.6 2.2 fusion.48
  231.9 2.5 convert_reduce_fusion.1
  234.4 27.7 %all-reduce = (f32[2,768]{1,0:T(2,128)}, f32[2,768]{1,0:T(2,128)}, f32[384]{0:T(512)}, f32[768]{0:T(1024)}, f32[768]{0:T(1024)}) all-reduce(f32[2,768]{1,0:T(2,128)S(1)} %pad_maximum_fusion.7, f32[2,768]{1,0:T(2,128)S(1)} %pad_maximum_fusion.8, f32[384]{0:T(512)S(1)} %reshape.311, ...), channel_id=1, replica_groups=mesh['dp'=2,'ctx'=4,'tp'=4] {'dp','ctx'}, use_global_device_ids=true, to_apply=%region_15.16 | all-reduce | flops 4992 | bytes 39936 | tf_op jit(solution)/shard_map/psum | solution.py:269
  262.1 4.9 %reduce-scatter.18.cloned.1.call-done = f32[96,768]{1,0:T(8,128)} async-done(((f32[768,768]{1,0:T(8,128)}), f32[96,768]{1,0:T(8,128)}) %reduce-scatter.18.cloned.1.call-update) | async-done | bytes 294928
  267.1 44.0 %reduce-scatter.12.cloned.1.call-done = f32[96,576]{1,0:T(8,128)} async-done(((f32[768,576]{1,0:T(8,128)}), f32[96,576]{1,0:T(8,128)}) %reduce-scatter.12.cloned.1.call-update) | async-done | bytes 221200 | tf_op jit(solution)/shard_map/reduce_scatter | solution.py:273
  (125 shorter events, 1.4 us)
Async XLA Ops:
  8.0 37.8 %copy-start = (bf16[1,256,768]{2,1,0:T(8,128)(2,1)S(1)}, bf16[1,256,768]{2,1,0:T(8,128)(2,1)}, u32[]{:S(2)}) copy-start(bf16[1,256,768]{2,1,0:T(8,128)(2,1)} %param.12) | copy-start | bytes 1179652
  8.0 37.2 %copy-start.29 = (f32[2,768]{1,0:T(2,128)S(1)}, f32[2,768]{1,0:T(2,128)}, u32[]{:S(2)}) copy-start(f32[2,768]{1,0:T(2,128)} %param.14) | copy-start | bytes 18436
  8.0 37.2 %copy-start.28 = (f32[2,768]{1,0:T(2,128)S(1)}, f32[2,768]{1,0:T(2,128)}, u32[]{:S(2)}) copy-start(f32[2,768]{1,0:T(2,128)} %param.15) | copy-start | bytes 18436
  8.0 95.4 %all-gather.3.cloned.1.call-start = ((), (), s32[]{:S(2)}) async-start(), calls=%async_computation.5 | async-start | bytes 1327104 | tf_op jit(solution)/shard_map/all_gather | solution.py:93
  8.8 96.6 %all-gather.5.cloned.1.call-start = ((), (), s32[]{:S(2)}) async-start(), calls=%async_computation.6 | async-start | bytes 1327104 | tf_op jit(solution)/shard_map/all_gather | solution.py:94
  9.5 121.7 %reduce-scatter.10.cloned.1.call-start = ((), (), s32[]{:S(2)}) async-start(), calls=%async_computation.7 | async-start | bytes 1966080 | tf_op jit(solution)/shard_map/reduce_scatter | solution.py:240
  10.7 35.7 %copy-start.18 = (f32[256]{0:T(256)}, f32[256]{0:T(256)S(1)}, u32[]{:S(2)}) copy-start(f32[256]{0:T(256)S(1)} %broadcast_multiply_fusion.4) | copy-start | bytes 3076
  12.0 34.4 %copy-start.21 = (f32[256]{0:T(256)}, f32[256]{0:T(256)S(1)}, u32[]{:S(2)}) copy-start(f32[256]{0:T(256)S(1)} %add_rsqrt_fusion) | copy-start | bytes 3076
  44.6 1.9 copy-start.31
  44.6 2.1 copy-start.33
  45.8 0.6 copy-start.13
  45.8 0.6 copy-start.24
  69.2 1.0 copy-start.17
  69.2 25.9 %copy-start.1 = (bf16[1,256,768]{2,1,0:T(8,128)(2,1)S(1)}, bf16[1,256,768]{2,1,0:T(8,128)(2,1)}, u32[]{:S(2)}) copy-start(bf16[1,256,768]{2,1,0:T(8,128)(2,1)} %param.23) | copy-start | bytes 1179652
  96.3 6.0 %copy-start.11 = (bf16[256,3,64]{0,2,1:T(8,128)(2,1)}, bf16[256,3,64]{0,2,1:T(8,128)(2,1)S(1)}, u32[]{:S(2)}) copy-start(bf16[256,3,64]{0,2,1:T(8,128)(2,1)S(1)} %get-tuple-element.159) | copy-start | bytes 294916
  97.5 1.2 copy-start.2
  100.0 3.4 %copy-start.15 = (f32[768]{0:T(1024)S(1)}, f32[768]{0:T(1024)}, u32[]{:S(2)}) copy-start(f32[768]{0:T(1024)} %get-tuple-element.163) | copy-start | bytes 9220
  100.0 3.4 %copy-start.19 = (f32[256]{0:T(256)S(1)}, f32[256]{0:T(256)}, u32[]{:S(2)}) copy-start(f32[256]{0:T(256)} %copy-done.18) | copy-start | bytes 3076
  100.1 3.4 %copy-start.22 = (f32[256]{0:T(256)S(1)}, f32[256]{0:T(256)}, u32[]{:S(2)}) copy-start(f32[256]{0:T(256)} %copy-done.21) | copy-start | bytes 3076
  100.1 3.4 %copy-start.26 = (f32[768]{0:T(1024)S(1)}, f32[768]{0:T(1024)}, u32[]{:S(2)}) copy-start(f32[768]{0:T(1024)} %get-tuple-element.118) | copy-start | bytes 9220
  100.1 3.4 %copy-start.32 = (f32[768]{0:T(1024)S(1)}, f32[768]{0:T(1024)}, u32[]{:S(2)}) copy-start(f32[768]{0:T(1024)} %param.20) | copy-start | bytes 9220
  100.1 129.5 %all-reduce.4.cloned.1.call-start = ((), (), s32[]{:S(2)}) async-start(), calls=%async_computation.12 | async-start | bytes 4718592 | tf_op jit(solution)/shard_map/psum | solution.py:164
  102.2 1.3 copy-start.7
  105.3 29.6 %copy-start.3 = (f32[256,768]{1,0:T(8,128)}, f32[256,768]{1,0:T(8,128)S(1)}, u32[]{:S(2)}) copy-start(f32[256,768]{1,0:T(8,128)S(1)} %convolution_add_fusion.1) | copy-start | bytes 2359300
  105.3 2.3 copy-start.10
  105.3 3.7 %copy-start.4 = (f32[256,768]{1,0:T(8,128)S(1)}, f32[256,768]{1,0:T(8,128)}, u32[]{:S(2)}) copy-start(f32[256,768]{1,0:T(8,128)} %fusion.93) | copy-start | bytes 2359300
  105.4 3.7 %copy-start.9 = (bf16[768,768]{1,0:T(8,128)(2,1)S(1)}, bf16[768,768]{1,0:T(8,128)(2,1)}, u32[]{:S(2)}) copy-start(bf16[768,768]{1,0:T(8,128)(2,1)} %all-gather.5.cloned.1.call-done) | copy-start | bytes 3538948
  133.4 1.5 copy-start.12
  134.9 1.6 copy-start.16
  134.9 1.6 copy-start.20
  134.9 1.6 copy-start.23
  134.9 1.6 copy-start.27
  134.9 127.2 %reduce-scatter.16.cloned.1.call-start = ((), (), s32[]{:S(2)}) async-start(), calls=%async_computation.10 | async-start | bytes 884736
  136.4 125.8 %reduce-scatter.14.cloned.1.call-start = ((), (), s32[]{:S(2)}) async-start(), calls=%async_computation.9 | async-start | bytes 2654208 | tf_op jit(solution)/shard_map/reduce_scatter | solution.py:275
  138.6 128.5 %reduce-scatter.18.cloned.1.call-start = ((), (), s32[]{:S(2)}) async-start(), calls=%async_computation.11 | async-start | bytes 2654208
  142.5 0.7 copy-start.14
  142.5 0.7 copy-start.25
  142.5 2.7 copy-start.8
  142.5 168.6 %reduce-scatter.12.cloned.1.call-start = ((), (), s32[]{:S(2)}) async-start(), calls=%async_computation.8 | async-start | bytes 2211840 | tf_op jit(solution)/shard_map/reduce_scatter | solution.py:273
  145.1 86.8 %copy-start.30 = (f32[768]{0:T(1024)S(1)}, f32[768]{0:T(1024)}, u32[]{:S(2)}) copy-start(f32[768]{0:T(1024)} %param.22) | copy-start | bytes 9220
  229.6 2.3 copy-start.5
  229.6 2.3 copy-start.6
Sparse Core Ops, SparseCore 0:
  10.7 31.4 all-gather.2
  44.1 25.0 all-gather.4
  139.4 34.9 reduce-scatter.15
  178.3 42.3 reduce-scatter.13
  224.4 42.6 reduce-scatter.17
  270.9 40.1 reduce-scatter.11
Sparse Core Ops, SparseCore 1:
  100.1 31.1 reduce-scatter.9
  135.0 94.5 all-reduce.3
where the time goes:
time: 319 us
  waiting for transfers between devices  155 us (49%)
  blocking collectives  106 us (33%)
  matrix products  22.4 us (7%)
  between operations  16.3 us (5%)
  other arithmetic  11.5 us (4%)
  local copies, waits for them, and re-layouts  6.53 us (2%)
    psum x1, waiting for transfers between devices, on_device(): branches = lax.psum(attn_part + mlp_part, 'tp')  84.1 us
    reduce_scatter x1, waiting for transfers between devices, on_device(): lax.psum_scatter(qkv_grad, ('dp', 'ctx'), scatter_dimension=0, tiled=True)  44 us
    all_gather x1, blocking collectives, on_device(): lax.all_gather(w_qkv, ('dp', 'ctx'), axis=0, tiled=True)  32.6 us
    psum x1, blocking collectives, on_device(): lax.psum((gain_part, bias_part, qv_grad, up_bias_grad, out_bias_grad), ('...  27.7 us
    all_gather x1, blocking collectives, on_device(): lax.all_gather(w_dense, ('dp', 'ctx'), axis=0, tiled=True)  24.9 us
    reduce_scatter x1, waiting for transfers between devices, on_device(): lax.psum_scatter(kv_terms.reshape(back_kv.shape[0], 2 * head_cols), 'ctx'...  20.8 us
    all_gather x1, blocking collectives, on_device(): lax.all_gather(kv_flat, 'ctx', axis=0, tiled=True)  20.8 us
    unnamed x10, waiting for transfers between devices  6.4 us
  transfers between devices with their start and end apart: 8, of which 4 were waited for; matrix products, arithmetic and copies ran while one was open for 11% of the time, Pallas kernels for 0%

commit v1 on v0

--- a/solution.py
+++ b/solution.py
@@ -1,8 +1,11 @@
+import functools
 import math
 
 import jax
 import jax.numpy as jnp
 from jax import lax
+from jax.experimental import pallas as pl
+from jax.experimental.pallas import tpu as pltpu
 from jax.sharding import PartitionSpec as P
 
 HD = 64
@@ -290,6 +293,478 @@
     )
 
 
+BF = jnp.bfloat16
+F32 = jnp.float32
+
+
+def mm(a, b, ca=1, cb=0):
+    return lax.dot_general(a, b, (((ca,), (cb,)), ((), ())), preferred_element_type=F32)
+
+
+def turn(x, cos_w, sin_a, sin_b):
+    width = x.shape[1]
+    return x * cos_w + pltpu.roll(x, width - ROT // 2, 1) * sin_a + pltpu.roll(x, ROT // 2, 1) * sin_b
+
+
+def block_kernel(
+    tp,
+    heads,
+    n_copies,
+    x_ref,
+    span_ref,
+    gain_ref,
+    shift_ref,
+    wqkv_ref,
+    qvb_ref,
+    wdense_ref,
+    wup_ref,
+    upb_ref,
+    wdown_ref,
+    outb_ref,
+    g_ref,
+    cos_ref,
+    sina_ref,
+    sinb_ref,
+    layer_out,
+    grad_in,
+    small_out,
+    qkv_out,
+    dense_out,
+    up_out,
+    down_out,
+    qkv_w,
+    dense_w,
+    up_w,
+    down_w,
+    kv_f,
+    xhat_s,
+    inv_s,
+    z1t_s,
+    z2t_s,
+    gt_s,
+    attn_t,
+    dq_t,
+    dkv_g,
+    dkv_bufs,
+    qkv_g,
+    qkv_bufs,
+    dense_g,
+    dense_bufs,
+    up_g,
+    up_bufs,
+    down_g,
+    down_bufs,
+    out_g,
+    out_snd,
+    out_rcv,
+    out_fin,
+    t_g,
+    t_snd,
+    t_rcv,
+    t_fin,
+    sm_z,
+    sm_p,
+    ssem,
+    rsem,
+):
+    c, t, z = lax.axis_index("dp"), lax.axis_index("ctx"), lax.axis_index("tp")
+    xi, yi = t % 2, t // 2
+    tx, ty, td = t + 1 - 2 * xi, t + 2 - 4 * yi, 3 - t
+    to_x, to_y, to_d, to_c = (c, tx, z), (c, ty, z), (c, td, z), (1 - c, t, z)
+    tok = x_ref.shape[0] * x_ref.shape[1]
+    feat = x_ref.shape[2]
+    spans = tok // SPAN
+    hc = heads * HD
+
+    barrier = pltpu.get_barrier_semaphore()
+    peers = [to_c, to_x, to_y, to_d] + [(1 - c, o, z) for o in (tx, ty, td)]
+    z_peers = [(c, t, (z + d) % tp) for d in range(1, tp)]
+    for dev in peers + z_peers:
+        pl.semaphore_signal(barrier, inc=1, device_id=dev, device_id_type=pl.DeviceIdType.MESH)
+    pl.semaphore_wait(barrier, len(peers + z_peers))
+
+    copies = []
+
+    def rcopy(src, dst, dev):
+        i = len(copies)
+        cp = pltpu.make_async_remote_copy(
+            src_ref=src,
+            dst_ref=dst,
+            send_sem=ssem.at[i],
+            recv_sem=rsem.at[i],
+            device_id=dev,
+            device_id_type=pl.DeviceIdType.MESH,
+        )
+        cp.start()
+        copies.append(cp)
+        return cp
+
+    class Gather:
+        def __init__(self, own, full, cores=True):
+            self.full, self.cores = full, cores
+            self.base = 4 * c if cores else 0
+            me = self.base + t
+            if own is None:
+                own = full.at[me]
+            else:
+                full[me] = own[...]
+            self.half = full.shape[1] // 2
+            self.cx = rcopy(own, full.at[me], to_x)
+            self.cy = rcopy(own, full.at[me], to_y)
+            self.cc = [rcopy(own, full.at[me], to_c)] if cores else []
+
+        def relay(self):
+            full, h = self.full, self.half
+            sx, sy = self.base + tx, self.base + ty
+            self.cx.wait_recv()
+            a = full.at[sx, pl.ds(0, h)]
+            self.d1 = rcopy(a, a, to_y)
+            if self.cores:
+                self.cc.append(rcopy(full.at[sx], full.at[sx], to_c))
+            self.cy.wait_recv()
+            b = full.at[sy, pl.ds(h, h)]
+            self.d2 = rcopy(b, b, to_x)
+            if self.cores:
+                self.cc.append(rcopy(full.at[sy], full.at[sy], to_c))
+
+        def finish(self):
+            sd = self.base + td
+            self.d1.wait_recv()
+            self.d2.wait_recv()
+            if self.cores:
+                self.cc.append(rcopy(self.full.at[sd], self.full.at[sd], to_c))
+                for cp in self.cc:
+                    cp.wait_recv()
+
+        def value(self):
+            s = self.full.shape
+            return self.full[...].reshape(s[0] * s[1], s[2])
+
+    class Scatter:
+        def __init__(self, total, bufs, cores=True):
+            self.g, self.b, self.cores = total, bufs, cores
+            self.h = total.shape[1] // 2
+            if cores:
+                snd, rcv = bufs[:2]
+                snd[...] = total[pl.ds(4 * (1 - c), 4)].astype(BF)
+                self.cc = rcopy(snd, rcv, to_c)
+
+        def first(self):
+            a1, b1, ra1, rb1 = self.b[2:6]
+            h = self.h
+            if self.cores:
+                self.cc.wait_recv()
+                self.s = self.g.at[pl.ds(4 * c, 4)]
+                self.s[...] = self.s[...] + self.b[1][...].astype(F32)
+            else:
+                self.s = self.g
+            for k in range(2):
+                a1[k] = self.s[2 * k + 1 - xi, pl.ds(0, h)].astype(BF)
+                b1[k] = self.s[2 * (1 - yi) + k, pl.ds(h, h)].astype(BF)
+            self.ca = rcopy(a1, ra1, to_x)
+            self.cb = rcopy(b1, rb1, to_y)
+
+        def second(self):
+            ra1, rb1, a2, b2, ra2, rb2 = self.b[4:10]
+            h = self.h
+            self.ca.wait_recv()
+            a2[...] = (self.s[2 * (1 - yi) + xi, pl.ds(0, h)] + ra1[1 - yi].astype(F32)).astype(BF)
+            self.ca2 = rcopy(a2, ra2, to_y)
+            self.cb.wait_recv()
+            b2[...] = (self.s[2 * yi + 1 - xi, pl.ds(h, h)] + rb1[1 - xi].astype(F32)).astype(BF)
+            self.cb2 = rcopy(b2, rb2, to_x)
+
+        def finish(self):
+            ra1, rb1, a2, b2, ra2, rb2 = self.b[4:10]
+            h = self.h
+            self.ca2.wait_recv()
+            top = self.s[t, pl.ds(0, h)] + ra1[yi].astype(F32) + ra2[...].astype(F32)
+            self.cb2.wait_recv()
+            low = self.s[t, pl.ds(h, h)] + rb1[xi].astype(F32) + rb2[...].astype(F32)
+            return top, low
+
+    def z_scatter(total, snd, rcv):
+        snd[...] = total[...].astype(BF)
+        return [rcopy(snd.at[(z + d) % tp], rcv.at[d - 1], (c, t, (z + d) % tp)) for d in range(1, tp)]
+
+    def z_sum(cps, total, rcv):
+        acc = total[z]
+        for d in range(1, tp):
+            cps[d - 1].wait_recv()
+            acc = acc + rcv[d - 1].astype(F32)
+        return acc
+
+    def z_gather(fin):
+        return [rcopy(fin.at[z], fin.at[z], dev) for dev in z_peers]
+
+    ag_qkv = Gather(wqkv_ref, qkv_w)
+    ag_dense = Gather(wdense_ref, dense_w)
+
+    x = x_ref[...].reshape(tok, feat).astype(F32)
+    cen = x - jnp.mean(x, axis=-1, keepdims=True)
+    inv = lax.rsqrt(jnp.mean(cen * cen, axis=-1, keepdims=True) + EPS)
+    xhat = cen * inv
+    xhat_s[...] = xhat.reshape(xhat_s.shape)
+    inv_s[...] = jnp.broadcast_to(inv, (tok, 128)).reshape(inv_s.shape)
+    z1 = (xhat * gain_ref[0:1, :] + shift_ref[0:1, :]).astype(BF)
+    z2 = (xhat * gain_ref[1:2, :] + shift_ref[1:2, :]).astype(BF)
+    g = g_ref[...].reshape(tok, feat)
+    sm_z[z] = jnp.zeros(sm_z.shape[1:], F32)
+    sm_p[4 * c + t] = jnp.zeros(sm_p.shape[1:], F32)
+
+    ag_qkv.relay()
+    ag_dense.relay()
+    ag_qkv.finish()
+    proj = mm(z1, ag_qkv.value())
+    wide = cos_ref.shape[1]
+    proj = jnp.concatenate([proj, jnp.zeros((tok, wide - proj.shape[1]), F32)], axis=1)
+    qkv = turn(proj + qvb_ref[...], cos_ref[...], sina_ref[...], sinb_ref[...])
+    queries = [(qkv[:, 192 * h : 192 * h + HD].astype(BF) * BF(0.125)) for h in range(heads)]
+    kv_f[t] = jnp.concatenate([qkv[:, 192 * h + HD : 192 * h + 192] for h in range(heads)], axis=1).astype(BF)
+    ag_kv = Gather(None, kv_f, cores=False)
+    ag_up = Gather(wup_ref, up_w)
+    ag_down = Gather(wdown_ref, down_w)
+    gt_s[...] = g.T
+    z1t_s[...] = z1.T
+    z2t_s[...] = z2.T
+    ag_dense.finish()
+    dattn = mm(g, ag_dense.value()).astype(BF)
+    dattn_t = dattn.T
+    ag_kv.relay()
+    ag_kv.finish()
+
+    lane = lax.broadcasted_iota(jnp.int32, (1, SPAN), 1)
+    own_pos = jnp.concatenate([span_ref[0, t * spans + i] * SPAN + lane for i in range(spans)], axis=1)
+    row = lax.broadcasted_iota(jnp.int32, (SPAN, 1), 0)
+    keys = 4 * tok
+    masks = jnp.concatenate(
+        [row + span_ref[0, i] * SPAN <= own_pos for i in range(keys // SPAN)], axis=0
+    )
+    for h in range(heads):
+        kvh = kv_f[:, :, 128 * h : 128 * h + 128].reshape(keys, 128)
+        k, v = kvh[:, :HD], kvh[:, HD:]
+        s = jnp.where(masks, mm(k, queries[h], 1, 1), NEG)
+        e = jnp.exp(s - jnp.max(s, axis=0, keepdims=True))
+        l_inv = 1.0 / jnp.sum(e, axis=0, keepdims=True)
+        o_t = (mm(v, e.astype(BF), 0, 0) * l_inv).astype(BF)
+        attn_t[h * HD : (h + 1) * HD, :] = o_t
+        da_t = dattn_t[h * HD : (h + 1) * HD, :]
+        delta = jnp.sum(da_t.astype(F32) * o_t.astype(F32), axis=0, keepdims=True)
+        p = e * l_inv
+        ds = (p * (mm(v, da_t) - delta)).astype(BF)
+        dq_t[h * HD : (h + 1) * HD, :] = mm(k, ds, 0, 0) * 0.125
+        dk = mm(ds, queries[h])
+        dv = mm(p.astype(BF), dattn[:, h * HD : (h + 1) * HD])
+        dkv_g[:, :, 128 * h : 128 * h + 128] = jnp.concatenate([dk, dv], axis=1).reshape(4, tok, 128)
+        if h == 0:
+            ag_up.relay()
+        if h == 1:
+            ag_down.relay()
+    rs_kv = Scatter(dkv_g, dkv_bufs, cores=False)
+    rs_kv.first()
+
+    attn = attn_t[...].T
+    dense_g[...] = mm(gt_s[...], attn).reshape(dense_g.shape)
+    rs_dense = Scatter(dense_g, dense_bufs)
+    ag_up.finish()
+    pre = mm(z2, ag_up.value()) + upb_ref[...]
+    phi = 0.5 * (1.0 + lax.erf(pre * (1.0 / math.sqrt(2.0))))
+    act = (pre * phi).astype(BF)
+    slope = phi + pre * jnp.exp(-0.5 * pre * pre) * (1.0 / math.sqrt(2.0 * math.pi))
+    ag_down.finish()
+    out_g[...] = (mm(attn, ag_dense.value(), 1, 1) + mm(act, ag_down.value(), 1, 1)).reshape(out_g.shape)
+    z_out = z_scatter(out_g, out_snd, out_rcv)
+    rs_kv.second()
+    down_g[...] = mm(gt_s[...], act).reshape(down_g.shape)
+    rs_down = Scatter(down_g, down_bufs)
+    dpre = mm(g, ag_down.value()) * slope
+    dpre_b = dpre.astype(BF)
+    rs_dense.first()
+    kv_top, kv_low = rs_kv.finish()
+    dkv = jnp.concatenate([kv_top, kv_low], axis=0)
+    dq = dq_t[...].T
+    parts = []
+    for h in range(heads):
+        parts += [dq[:, h * HD : (h + 1) * HD], dkv[:, 128 * h : 128 * h + 128]]
+    parts.append(jnp.zeros((tok, wide - 3 * hc), F32))
+    dproj = turn(jnp.concatenate(parts, axis=1), cos_ref[...], -sina_ref[...], -sinb_ref[...])
+    dproj_b = dproj.astype(BF)[:, : 3 * hc]
+    dz1 = mm(dproj_b, ag_qkv.value(), 1, 1)
+    dz2 = mm(dpre_b, ag_up.value(), 1, 1)
+    t_g[...] = (dz1 * gain_ref[0:1, :] + dz2 * gain_ref[1:2, :]).reshape(t_g.shape)
+    z_t = z_scatter(t_g, t_snd, t_rcv)
+    xhat = xhat_s[...].reshape(tok, feat)
+    sm_z[z, 0:1, :] = jnp.sum(dz1 * xhat, axis=0, keepdims=True)
+    sm_z[z, 1:2, :] = jnp.sum(dz2 * xhat, axis=0, keepdims=True)
+    sm_z[z, 2:3, :] = jnp.sum(dz1, axis=0, keepdims=True)
+    sm_z[z, 3:4, :] = jnp.sum(dz2, axis=0, keepdims=True)
+    c_sm = z_gather(sm_z)
+    rs_down.first()
+    up_g[...] = mm(z2t_s[...], dpre_b).reshape(up_g.shape)
+    rs_up = Scatter(up_g, up_bufs)
+    qkv_g[...] = mm(z1t_s[...], dproj_b).reshape(qkv_g.shape)
+    rs_qkv = Scatter(qkv_g, qkv_bufs)
+    rs_dense.second()
+    fin = z_sum(z_out, out_g, out_rcv)
+    out_fin[z] = (x_ref[z].astype(F32) + outb_ref[...] + fin).astype(BF)
+    c_out = z_gather(out_fin)
+    rs_up.first()
+    rs_qkv.first()
+    for cp in c_sm:
+        cp.wait_recv()
+    me = 4 * c + t
+    sm = sm_z[0]
+    for i in range(1, tp):
+        sm = sm + sm_z[i]
+    sm_p[me] = sm
+    sm_p[me, 4:5, :] = jnp.sum(g.astype(F32), axis=0, keepdims=True)
+    sm_p[me, 5:6, 0 : dpre.shape[1]] = jnp.sum(dpre, axis=0, keepdims=True)
+    sm_p[me, 6:7, 0:wide] = jnp.sum(dproj, axis=0, keepdims=True)
+    c_pl = [rcopy(sm_p.at[me], sm_p.at[me], dev) for dev in peers]
+    rs_down.second()
+    tt = z_sum(z_t, t_g, t_rcv)
+    xh = xhat_s[z]
+    back = inv_s[z, :, 0:1] * (
+        tt - jnp.mean(tt, axis=-1, keepdims=True) - xh * jnp.mean(tt * xh, axis=-1, keepdims=True)
+    )
+    t_fin[z] = (g_ref[z].astype(F32) + back).astype(BF)
+    c_t = z_gather(t_fin)
+    rs_up.second()
+    rs_qkv.second()
+    for rs, out in ((rs_dense, dense_out), (rs_down, down_out), (rs_up, up_out), (rs_qkv, qkv_out)):
+        top, low = rs.finish()
+        out[pl.ds(0, rs.h), :] = top
+        out[pl.ds(rs.h, rs.h), :] = low
+    for cp in c_pl:
+        cp.wait_recv()
+    sm = sm_p[0]
+    for i in range(1, 8):
+        sm = sm + sm_p[i]
+    small_out[...] = sm
+    for cp in c_out:
+        cp.wait_recv()
+    layer_out[...] = out_fin[...]
+    for cp in c_t:
+        cp.wait_recv()
+    grad_in[...] = t_fin[...]
+    assert len(copies) <= n_copies
+    for cp in copies:
+        cp.wait_send()
+
+
+def one_kernel(tp, *args):
+    x, span, gains, shifts, wqkv, qvb, wdense, wup, upb, wdown, outb, g = args
+    tok, feat = x.shape[1:]
+    rows = wqkv.shape[0]
+    heads = qvb.shape[0] // (2 * HD)
+    ff = wup.shape[1]
+    spans = tok // SPAN
+    wide = -(-3 * heads * HD // 128) * 128
+    own = lax.dynamic_slice_in_dim(span[0], lax.axis_index("ctx") * spans, spans)
+    pos = (own[:, None] * SPAN + jnp.arange(SPAN, dtype=jnp.int32)[None, :]).reshape(-1)
+    cos_t, sin_t = rotary_tables(pos, ROT)
+    col = jnp.arange(wide) % (3 * HD)
+    turned = (col < 2 * HD) & (jnp.arange(wide) < 3 * heads * HD)
+    low = turned & (col % HD < ROT // 2)
+    high = turned & (col % HD >= ROT // 2) & (col % HD < ROT)
+    reps = wide // (ROT // 2)
+    cos_w = jnp.where(low | high, jnp.tile(cos_t, (1, reps)), 1.0)
+    sin_w = jnp.tile(sin_t, (1, reps))
+    sin_a = jnp.where(low, -sin_w, 0.0)
+    sin_b = jnp.where(high, sin_w, 0.0)
+    pair = qvb.reshape(heads, 2, HD)
+    bias = jnp.stack([pair[:, 0], jnp.zeros_like(pair[:, 0]), pair[:, 1]], axis=1).reshape(1, -1)
+    bias = jnp.pad(bias, ((0, 0), (0, wide - bias.shape[1])))
+    piece = tok // tp
+    cols = (wqkv.shape[1], wdense.shape[1], ff, ff)
+    kvw = 2 * heads * HD
+
+    def bufs(r, w, cores=True):
+        h = r // 2
+        first = [pltpu.VMEM((4, r, w), BF)] * 2 if cores else [pltpu.VMEM((8, 128), F32)] * 2
+        return tuple(first + [pltpu.VMEM((2, h, w), BF)] * 4 + [pltpu.VMEM((h, w), BF)] * 4)
+
+    vm = pltpu.VMEM
+    scratch = [vm((8, rows, w), BF) for w in cols]
+    scratch += [
+        vm((4, tok, kvw), BF),
+        vm((tp, piece, feat), F32),
+        vm((tp, piece, 128), F32),
+        vm((feat, tok), BF),
+        vm((feat, tok), BF),
+        vm((feat, tok), BF),
+        vm((heads * HD, tok), BF),
+        vm((heads * HD, tok), F32),
+        vm((4, tok, kvw), F32),
+        bufs(tok, kvw, False),
+    ]
+    for w in cols:
+        scratch += [vm((8, rows, w), F32), bufs(rows, w)]
+    for i in range(2):
+        scratch += [
+            vm((tp, piece, feat), F32),
+            vm((tp, piece, feat), BF),
+            vm((tp - 1, piece, feat), BF),
+            vm((tp, piece, feat), BF),
+        ]
+    n_copies = 128
+    scratch += [
+        vm((tp, 8, feat), F32),
+        vm((8, 8, feat), F32),
+        pltpu.SemaphoreType.DMA((n_copies,)),
+        pltpu.SemaphoreType.DMA((n_copies,)),
+    ]
+    vspec = pl.BlockSpec(memory_space=pltpu.VMEM)
+    specs = [vspec] * 15
+    specs[1] = pl.BlockSpec(memory_space=pltpu.SMEM)
+    sds = jax.ShapeDtypeStruct
+    layer_out, grad_in, small, gqkv, gdense, gup, gdown = pl.pallas_call(
+        functools.partial(block_kernel, tp, heads, n_copies),
+        out_shape=(
+            sds((tp, piece, feat), BF),
+            sds((tp, piece, feat), BF),
+            sds((8, feat), F32),
+        )
+        + tuple(sds((rows, w), F32) for w in cols),
+        in_specs=specs,
+        out_specs=tuple([vspec] * 7),
+        scratch_shapes=scratch,
+        compiler_params=pltpu.CompilerParams(
+            collective_id=0, has_side_effects=True, vmem_limit_bytes=60 * 1024 * 1024
+        ),
+    )(
+        x.reshape(tp, piece, feat),
+        span,
+        gains,
+        shifts,
+        wqkv,
+        bias,
+        wdense,
+        wup,
+        upb[None],
+        wdown,
+        outb[None],
+        g.reshape(tp, piece, feat),
+        cos_w,
+        sin_a,
+        sin_b,
+    )
+    qv = small[6, : 3 * heads * HD].reshape(heads, 3, HD)[:, 0::2].reshape(-1)
+    return (
+        layer_out.reshape(1, tok, feat),
+        grad_in.reshape(1, tok, feat),
+        small[0:2],
+        small[2:4],
+        gqkv,
+        qv,
+        gdense,
+        gup,
+        small[5, :ff],
+        gdown,
+        small[4],
+    )
+
+
 def solution(mesh):
     placed = (
         P("dp", "ctx", None),
@@ -305,8 +780,12 @@
         P(),
         P("dp", "ctx", None),
     )
+    sizes = dict(mesh.shape)
+    body = on_device
+    if sizes["dp"] == 2 and sizes["ctx"] == 4:
+        body = functools.partial(one_kernel, sizes["tp"])
     return jax.shard_map(
-        on_device,
+        body,
         mesh=mesh,
         in_specs=placed,
         out_specs=(

time: 319 us -> 97.1 us (0.30)
  waiting for transfers between devices: 155 us -> 0 us
  blocking collectives: 106 us -> 0 us
  Pallas kernels: 0 us -> 80.3 us
  matrix products: 22.4 us -> 0 us
  between operations: 16.3 us -> 0.73 us
  other arithmetic: 11.5 us -> 2.47 us
  local copies, waits for them, and re-layouts: 6.53 us -> 13.2 us
    psum x1 -> x0, waiting for transfers between devices: 84.1 us -> none  [on_device(): branches = lax.psum(attn_part + mlp_part, 'tp')]
    pallas_call x0 -> x1, Pallas kernels: none -> 80.3 us  [one_kernel(): pl.pallas_call(functools.partial(block_kernel, tp, heads, n_copies), out_...]
    all_gather x3 -> x0, blocking collectives: 78.2 us -> none  [the longest x1 32.6 us: on_device(): lax.all_gather(w_qkv, ('dp', 'ctx'), axis=0, tiled=True)]
    reduce_scatter x3 -> x0, waiting for transfers between devices: 64.8 us -> none  [the longest x1 44 us: on_device(): lax.psum_scatter(qkv_grad, ('dp', 'ctx'), scatter_dimension=0, tiled=True)]
    psum x1 -> x0, blocking collectives: 27.7 us -> none  [on_device(): lax.psum((gain_part, bias_part, qv_grad, up_bias_grad, out_bias_grad), ('...]
    dot_general x18 -> x0, matrix products: 22.4 us -> none  [the longest x1 2.26 us: on_device(): jnp.dot(cotangent, full_down, preferred_element_type=jnp.float32)]
    reduce_sum x7 -> x0, other arithmetic: 9.28 us -> none  [the longest x1 2.54 us: on_device(): out_bias_grad = jnp.sum(cot_float, axis=0)]
    unnamed x10 -> x0, waiting for transfers between devices: 6.4 us -> none
  transfers between devices with their start and end apart: 8 -> 0, of which waited for: 4 -> 0; matrix products, arithmetic and copies ran while one was open for 11% -> 0% of each run, Pallas kernels for 0% -> 0%
where the time goes in v1:
time: 97.1 us; the launch traced here: 96.7 us
  Pallas kernels  80.3 us (83%)
  local copies, waits for them, and re-layouts  13.2 us (14%)
  other arithmetic  2.47 us (3%)
    pallas_call x1, Pallas kernels, one_kernel(): pl.pallas_call(functools.partial(block_kernel, tp, heads, n_copies), out_...  80.3 us
    unnamed x26, local copies, waits for them, and re-layouts  7.84 us

profile of v1, /device:TPU:0, one launch (start us, length us, event | category | flops | bytes accessed | tf_op | source)
XLA Modules:
  0.0 96.7 jit_solution(9507337868253799825)
XLA Ops:
  0.6 0.0 copy-start.9
  0.7 0.6 copy-done.9
  1.3 0.1 multiply_bitcast_fusion
  1.4 0.1 convert_bitcast_fusion
  1.5 0.1 pad.6.clone
  1.6 0.0 copy-start.8
  1.6 0.7 copy-done.8
  2.3 0.1 reshape.135
  2.4 0.1 pad_maximum_fusion
  2.4 0.1 reshape.136
  2.5 0.0 copy-start.6
  2.5 0.6 pad.4.qvb_ref
  3.1 0.1 copy-done.6
  3.2 0.0 copy-start.7
  3.2 0.6 broadcast_in_dim.28.upb_ref
  3.8 0.1 copy-done.7
  3.9 0.6 broadcast_in_dim.29.outb_ref
  4.5 0.1 multiply_sine_fusion
  4.6 0.1 broadcast_bitcast_fusion
  4.7 0.2 copy.24
  4.9 1.2 %broadcast_select_fusion = (f32[256,640]{1,0:T(8,128)}, f32[256,640]{1,0:T(8,128)}) fusion(f32[256,640]{1,0:T(8,128)S(1)} %copy.24, pred[640]{0:T(1024)(128)(4,1)S(1)} %get-tuple-element.37, pred[640]{0:T(1024)(128)(4,1)S(1)} %get-tuple-element.38), kind=kLoop, calls=%fused_computation.1 | loop fusion | flops 491520 | bytes 1967360 | tf_op jit(solution)/shard_map/jit(_where)/select_n | solution.py:674
  6.1 0.2 copy.23
  6.4 0.9 broadcast_select_fusion.1.cos_ref
  7.3 80.3 %shard_map.203 = (bf16[4,64,768]{2,1,0:T(8,128)(2,1)}, bf16[4,64,768]{2,1,0:T(8,128)(2,1)}, f32[8,768]{1,0:T(8,128)}, f32[96,576]{1,0:T(8,128)}, f32[96,192]{1,0...) custom-call(bf16[4,64,768]{2,1,0:T(8,128)(2,1)} %bitcast.13, s32[1,8]{1,0:T(1,128)} %span_ref.1, f32[2,768]{1,0:T(2,128)} %gain_ref.1, ...), custom_call_target="tpu_custom_call" | custom-call | tf_op jit(solution)/shard_map/pallas_call | solution.py:721
  87.6 0.0 copy-start.5
  87.6 0.8 slice_reduce_fusion.2
  88.4 0.1 reshape_squeeze.3
  88.5 0.7 reshape.140
  89.2 0.0 copy-done.5
  89.2 0.6 slice_reduce_fusion
  89.8 0.6 fusion.7
  90.4 0.0 copy-start
  90.4 1.8 %copy.32 = bf16[1,256,768]{2,1,0:T(8,128)(2,1)} copy(bf16[1,256,768]{2,1,0:T(8,128)(2,1)} %bitcast.16) | data formatting | bytes 786432
  92.2 0.0 copy-done
  92.2 0.0 copy-start.3
  92.2 0.7 copy.33
  93.0 0.3 copy-done.3
  93.3 0.0 copy-start.4
  93.3 0.0 copy-start.2
  93.3 0.7 copy.34
  94.0 0.3 copy-done.4
  94.3 0.6 copy.35
  94.9 0.0 copy-done.2
  94.9 0.0 copy-start.1
  94.9 0.7 copy.36
  95.6 0.4 copy-done.1
  96.0 0.7 copy.37
  (5 shorter events, 0.1 us)
Async XLA Ops:
  0.6 0.7 copy-start.9
  1.6 0.7 copy-start.8
  2.5 0.7 copy-start.6
  3.2 0.7 copy-start.7
  87.6 1.6 %copy-start.5 = (f32[8,768]{1,0:T(8,128)S(1)}, f32[8,768]{1,0:T(8,128)}, u32[]{:S(2)}) copy-start(f32[8,768]{1,0:T(8,128)} %get-tuple-element.20) | copy-start | bytes 73732
  90.4 1.8 %copy-start = (bf16[4,64,768]{2,1,0:T(8,128)(2,1)S(1)}, bf16[4,64,768]{2,1,0:T(8,128)(2,1)}, u32[]{:S(2)}) copy-start(bf16[4,64,768]{2,1,0:T(8,128)(2,1)} %get-tuple-element.19) | copy-start | bytes 1179652
  92.2 1.1 %copy-start.3 = (f32[96,576]{1,0:T(8,128)S(1)}, f32[96,576]{1,0:T(8,128)}, u32[]{:S(2)}) copy-start(f32[96,576]{1,0:T(8,128)} %get-tuple-element.54) | copy-start | bytes 663556
  93.3 1.0 copy-start.4
  93.3 1.6 %copy-start.2 = (f32[96,768]{1,0:T(8,128)S(1)}, f32[96,768]{1,0:T(8,128)}, u32[]{:S(2)}) copy-start(f32[96,768]{1,0:T(8,128)} %get-tuple-element.57) | copy-start | bytes 884740
  94.9 1.1 %copy-start.1 = (f32[96,768]{1,0:T(8,128)S(1)}, f32[96,768]{1,0:T(8,128)}, u32[]{:S(2)}) copy-start(f32[96,768]{1,0:T(8,128)} %get-tuple-element.59) | copy-start | bytes 884740

commit v2 on v1

--- a/solution.py
+++ b/solution.py
@@ -322,9 +322,6 @@
     wdown_ref,
     outb_ref,
     g_ref,
-    cos_ref,
-    sina_ref,
-    sinb_ref,
     layer_out,
     grad_in,
     small_out,
@@ -364,6 +361,9 @@
     t_fin,
     sm_z,
     sm_p,
+    cos_ref,
+    sina_ref,
+    sinb_ref,
     ssem,
     rsem,
 ):
@@ -509,33 +509,60 @@
     z1 = (xhat * gain_ref[0:1, :] + shift_ref[0:1, :]).astype(BF)
     z2 = (xhat * gain_ref[1:2, :] + shift_ref[1:2, :]).astype(BF)
     g = g_ref[...].reshape(tok, feat)
+    lane = lax.broadcasted_iota(jnp.int32, (1, SPAN), 1)
+    row = lax.broadcasted_iota(jnp.int32, (SPAN, 1), 0)
+    wide = -(-3 * hc // 128) * 128
+    col_pos = jnp.concatenate([span_ref[0, t * spans + i] * SPAN + row for i in range(spans)], axis=0)
+    freq = jnp.zeros((1, 128), F32)
+    for f in range(ROT // 2):
+        step = 1.0 / 10000.0 ** (f * 2.0 / ROT)
+        freq = jnp.where(lane % (ROT // 2) == f, step, freq)
+    angle = col_pos.astype(F32) * freq
+    reps = wide // 128
+    cos_w = jnp.concatenate([jnp.cos(angle)] * reps, axis=1)
+    sin_w = jnp.concatenate([jnp.sin(angle)] * reps, axis=1)
+    col = lax.broadcasted_iota(jnp.int32, (1, wide), 1)
+    turned = (col % (3 * HD) < 2 * HD) & (col < 3 * hc)
+    lo = turned & (col % HD < ROT // 2)
+    hi = turned & (col % HD >= ROT // 2) & (col % HD < ROT)
+    cos_ref[...] = jnp.where(lo | hi, cos_w, 1.0)
+    sina_ref[...] = jnp.where(lo, -sin_w, 0.0)
+    sinb_ref[...] = jnp.where(hi, sin_w, 0.0)
+    qvb = qvb_ref[...].reshape(1, 2 * hc)
+    bias = []
+    for h in range(heads):
+        bias += [qvb[:, 128 * h : 128 * h + HD], jnp.zeros((1, HD), F32), qvb[:, 128 * h + HD : 128 * h + 128]]
+    bias = jnp.concatenate(bias + [jnp.zeros((1, wide - 3 * hc), F32)], axis=1)
     sm_z[z] = jnp.zeros(sm_z.shape[1:], F32)
     sm_p[4 * c + t] = jnp.zeros(sm_p.shape[1:], F32)
 
     ag_qkv.relay()
+    ag_up = Gather(wup_ref, up_w)
     ag_dense.relay()
     ag_qkv.finish()
     proj = mm(z1, ag_qkv.value())
-    wide = cos_ref.shape[1]
     proj = jnp.concatenate([proj, jnp.zeros((tok, wide - proj.shape[1]), F32)], axis=1)
-    qkv = turn(proj + qvb_ref[...], cos_ref[...], sina_ref[...], sinb_ref[...])
+    qkv = turn(proj + bias, cos_ref[...], sina_ref[...], sinb_ref[...])
     queries = [(qkv[:, 192 * h : 192 * h + HD].astype(BF) * BF(0.125)) for h in range(heads)]
     kv_f[t] = jnp.concatenate([qkv[:, 192 * h + HD : 192 * h + 192] for h in range(heads)], axis=1).astype(BF)
     ag_kv = Gather(None, kv_f, cores=False)
-    ag_up = Gather(wup_ref, up_w)
-    ag_down = Gather(wdown_ref, down_w)
-    gt_s[...] = g.T
-    z1t_s[...] = z1.T
-    z2t_s[...] = z2.T
     ag_dense.finish()
     dattn = mm(g, ag_dense.value()).astype(BF)
     dattn_t = dattn.T
+    gt_s[...] = g.T
     ag_kv.relay()
+    ag_up.relay()
+    ag_down = Gather(wdown_ref, down_w)
+    z1t_s[...] = z1.T
+    z2t_s[...] = z2.T
+    ag_up.finish()
+    pre = mm(z2, ag_up.value()) + upb_ref[...].reshape(1, -1)
+    phi = 0.5 * (1.0 + lax.erf(pre * (1.0 / math.sqrt(2.0))))
+    act = (pre * phi).astype(BF)
+    slope = phi + pre * jnp.exp(-0.5 * pre * pre) * (1.0 / math.sqrt(2.0 * math.pi))
     ag_kv.finish()
 
-    lane = lax.broadcasted_iota(jnp.int32, (1, SPAN), 1)
     own_pos = jnp.concatenate([span_ref[0, t * spans + i] * SPAN + lane for i in range(spans)], axis=1)
-    row = lax.broadcasted_iota(jnp.int32, (SPAN, 1), 0)
     keys = 4 * tok
     masks = jnp.concatenate(
         [row + span_ref[0, i] * SPAN <= own_pos for i in range(keys // SPAN)], axis=0
@@ -557,29 +584,25 @@
         dv = mm(p.astype(BF), dattn[:, h * HD : (h + 1) * HD])
         dkv_g[:, :, 128 * h : 128 * h + 128] = jnp.concatenate([dk, dv], axis=1).reshape(4, tok, 128)
         if h == 0:
-            ag_up.relay()
-        if h == 1:
             ag_down.relay()
     rs_kv = Scatter(dkv_g, dkv_bufs, cores=False)
     rs_kv.first()
-
+    ag_down.finish()
     attn = attn_t[...].T
+    out_g[...] = (mm(attn, ag_dense.value(), 1, 1) + mm(act, ag_down.value(), 1, 1)).reshape(out_g.shape)
+    z_out = z_scatter(out_g, out_snd, out_rcv)
+    down_g[...] = mm(gt_s[...], act).reshape(down_g.shape)
+    rs_down = Scatter(down_g, down_bufs)
     dense_g[...] = mm(gt_s[...], attn).reshape(dense_g.shape)
     rs_dense = Scatter(dense_g, dense_bufs)
-    ag_up.finish()
-    pre = mm(z2, ag_up.value()) + upb_ref[...]
-    phi = 0.5 * (1.0 + lax.erf(pre * (1.0 / math.sqrt(2.0))))
-    act = (pre * phi).astype(BF)
-    slope = phi + pre * jnp.exp(-0.5 * pre * pre) * (1.0 / math.sqrt(2.0 * math.pi))
-    ag_down.finish()
-    out_g[...] = (mm(attn, ag_dense.value(), 1, 1) + mm(act, ag_down.value(), 1, 1)).reshape(out_g.shape)
-    z_out = z_scatter(out_g, out_snd, out_rcv)
     rs_kv.second()
-    down_g[...] = mm(gt_s[...], act).reshape(down_g.shape)
-    rs_down = Scatter(down_g, down_bufs)
+    rs_down.first()
+    rs_dense.first()
     dpre = mm(g, ag_down.value()) * slope
     dpre_b = dpre.astype(BF)
-    rs_dense.first()
+    up_g[...] = mm(z2t_s[...], dpre_b).reshape(up_g.shape)
+    rs_up = Scatter(up_g, up_bufs)
+    dz2 = mm(dpre_b, ag_up.value(), 1, 1)
     kv_top, kv_low = rs_kv.finish()
     dkv = jnp.concatenate([kv_top, kv_low], axis=0)
     dq = dq_t[...].T
@@ -590,26 +613,24 @@
     dproj = turn(jnp.concatenate(parts, axis=1), cos_ref[...], -sina_ref[...], -sinb_ref[...])
     dproj_b = dproj.astype(BF)[:, : 3 * hc]
     dz1 = mm(dproj_b, ag_qkv.value(), 1, 1)
-    dz2 = mm(dpre_b, ag_up.value(), 1, 1)
     t_g[...] = (dz1 * gain_ref[0:1, :] + dz2 * gain_ref[1:2, :]).reshape(t_g.shape)
     z_t = z_scatter(t_g, t_snd, t_rcv)
+    qkv_g[...] = mm(z1t_s[...], dproj_b).reshape(qkv_g.shape)
+    rs_qkv = Scatter(qkv_g, qkv_bufs)
+    fin = z_sum(z_out, out_g, out_rcv)
+    out_fin[z] = (x_ref[z].astype(F32) + outb_ref[...].reshape(1, -1) + fin).astype(BF)
+    c_out = z_gather(out_fin)
+    rs_up.first()
+    rs_down.second()
+    rs_dense.second()
     xhat = xhat_s[...].reshape(tok, feat)
     sm_z[z, 0:1, :] = jnp.sum(dz1 * xhat, axis=0, keepdims=True)
     sm_z[z, 1:2, :] = jnp.sum(dz2 * xhat, axis=0, keepdims=True)
     sm_z[z, 2:3, :] = jnp.sum(dz1, axis=0, keepdims=True)
     sm_z[z, 3:4, :] = jnp.sum(dz2, axis=0, keepdims=True)
     c_sm = z_gather(sm_z)
-    rs_down.first()
-    up_g[...] = mm(z2t_s[...], dpre_b).reshape(up_g.shape)
-    rs_up = Scatter(up_g, up_bufs)
-    qkv_g[...] = mm(z1t_s[...], dproj_b).reshape(qkv_g.shape)
-    rs_qkv = Scatter(qkv_g, qkv_bufs)
-    rs_dense.second()
-    fin = z_sum(z_out, out_g, out_rcv)
-    out_fin[z] = (x_ref[z].astype(F32) + outb_ref[...] + fin).astype(BF)
-    c_out = z_gather(out_fin)
-    rs_up.first()
     rs_qkv.first()
+    rs_up.second()
     for cp in c_sm:
         cp.wait_recv()
     me = 4 * c + t
@@ -621,7 +642,6 @@
     sm_p[me, 5:6, 0 : dpre.shape[1]] = jnp.sum(dpre, axis=0, keepdims=True)
     sm_p[me, 6:7, 0:wide] = jnp.sum(dproj, axis=0, keepdims=True)
     c_pl = [rcopy(sm_p.at[me], sm_p.at[me], dev) for dev in peers]
-    rs_down.second()
     tt = z_sum(z_t, t_g, t_rcv)
     xh = xhat_s[z]
     back = inv_s[z, :, 0:1] * (
@@ -629,7 +649,6 @@
     )
     t_fin[z] = (g_ref[z].astype(F32) + back).astype(BF)
     c_t = z_gather(t_fin)
-    rs_up.second()
     rs_qkv.second()
     for rs, out in ((rs_dense, dense_out), (rs_down, down_out), (rs_up, up_out), (rs_qkv, qkv_out)):
         top, low = rs.finish()
@@ -652,29 +671,31 @@
         cp.wait_send()
 
 
+def settle_kernel(heads, lay, gin, small, gqkv, gdense, gup, gdown, *outs):
+    o_lay, o_gin, o_gain, o_shift, o_qkv, o_qv, o_dense, o_up, o_upb, o_down, o_outb = outs
+    o_lay[...] = lay[...].reshape(o_lay.shape)
+    o_gin[...] = gin[...].reshape(o_gin.shape)
+    o_gain[...] = small[0:2, :]
+    o_shift[...] = small[2:4, :]
+    o_qkv[...] = gqkv[...]
+    o_dense[...] = gdense[...]
+    o_up[...] = gup[...]
+    o_down[...] = gdown[...]
+    o_outb[...] = small[4:5, :].reshape(o_outb.shape)
+    o_upb[...] = small[5:6, 0 : o_upb.shape[0]].reshape(o_upb.shape)
+    qv = []
+    for h in range(heads):
+        qv += [small[6:7, 192 * h : 192 * h + HD], small[6:7, 192 * h + 2 * HD : 192 * h + 192]]
+    o_qv[...] = jnp.concatenate(qv, axis=1).reshape(o_qv.shape)
+
+
 def one_kernel(tp, *args):
     x, span, gains, shifts, wqkv, qvb, wdense, wup, upb, wdown, outb, g = args
     tok, feat = x.shape[1:]
     rows = wqkv.shape[0]
     heads = qvb.shape[0] // (2 * HD)
     ff = wup.shape[1]
-    spans = tok // SPAN
     wide = -(-3 * heads * HD // 128) * 128
-    own = lax.dynamic_slice_in_dim(span[0], lax.axis_index("ctx") * spans, spans)
-    pos = (own[:, None] * SPAN + jnp.arange(SPAN, dtype=jnp.int32)[None, :]).reshape(-1)
-    cos_t, sin_t = rotary_tables(pos, ROT)
-    col = jnp.arange(wide) % (3 * HD)
-    turned = (col < 2 * HD) & (jnp.arange(wide) < 3 * heads * HD)
-    low = turned & (col % HD < ROT // 2)
-    high = turned & (col % HD >= ROT // 2) & (col % HD < ROT)
-    reps = wide // (ROT // 2)
-    cos_w = jnp.where(low | high, jnp.tile(cos_t, (1, reps)), 1.0)
-    sin_w = jnp.tile(sin_t, (1, reps))
-    sin_a = jnp.where(low, -sin_w, 0.0)
-    sin_b = jnp.where(high, sin_w, 0.0)
-    pair = qvb.reshape(heads, 2, HD)
-    bias = jnp.stack([pair[:, 0], jnp.zeros_like(pair[:, 0]), pair[:, 1]], axis=1).reshape(1, -1)
-    bias = jnp.pad(bias, ((0, 0), (0, wide - bias.shape[1])))
     piece = tok // tp
     cols = (wqkv.shape[1], wdense.shape[1], ff, ff)
     kvw = 2 * heads * HD
@@ -711,11 +732,14 @@
     scratch += [
         vm((tp, 8, feat), F32),
         vm((8, 8, feat), F32),
+        vm((tok, wide), F32),
+        vm((tok, wide), F32),
+        vm((tok, wide), F32),
         pltpu.SemaphoreType.DMA((n_copies,)),
         pltpu.SemaphoreType.DMA((n_copies,)),
     ]
     vspec = pl.BlockSpec(memory_space=pltpu.VMEM)
-    specs = [vspec] * 15
+    specs = [vspec] * 12
     specs[1] = pl.BlockSpec(memory_space=pltpu.SMEM)
     sds = jax.ShapeDtypeStruct
     layer_out, grad_in, small, gqkv, gdense, gup, gdown = pl.pallas_call(
@@ -738,31 +762,34 @@
         gains,
         shifts,
         wqkv,
-        bias,
+        qvb,
         wdense,
         wup,
-        upb[None],
+        upb,
         wdown,
-        outb[None],
+        outb,
         g.reshape(tp, piece, feat),
-        cos_w,
-        sin_a,
-        sin_b,
-    )
-    qv = small[6, : 3 * heads * HD].reshape(heads, 3, HD)[:, 0::2].reshape(-1)
-    return (
-        layer_out.reshape(1, tok, feat),
-        grad_in.reshape(1, tok, feat),
-        small[0:2],
-        small[2:4],
-        gqkv,
-        qv,
-        gdense,
-        gup,
-        small[5, :ff],
-        gdown,
-        small[4],
-    )
+    )
+    pieces = (layer_out, grad_in, small, gqkv, gdense, gup, gdown)
+    out = pl.pallas_call(
+        functools.partial(settle_kernel, heads),
+        out_shape=(
+            sds((1, tok, feat), BF),
+            sds((1, tok, feat), BF),
+            sds((2, feat), F32),
+            sds((2, feat), F32),
+            sds(gqkv.shape, F32),
+            sds((2 * heads * HD,), F32),
+            sds(gdense.shape, F32),
+            sds(gup.shape, F32),
+            sds((ff,), F32),
+            sds(gdown.shape, F32),
+            sds((feat,), F32),
+        ),
+        in_specs=[vspec] * 7,
+        out_specs=tuple([vspec] * 11),
+    )(*pieces)
+    return tuple(out)
 
 
 def solution(mesh):

time: 97.1 us -> 81.9 us (0.84)
  local copies, waits for them, and re-layouts: 13.2 us -> 0 us
  other arithmetic: 2.47 us -> 0 us
    unnamed x26 -> x0, local copies, waits for them, and re-layouts: 7.84 us -> none
    pallas_call x0 -> x1, Pallas kernels: none -> 2.69 us  [one_kernel(): pl.pallas_call(functools.partial(settle_kernel, heads), out_shape=(sds((1...]
    select_n x2 -> x0, other arithmetic: 2.08 us -> none  [the longest x1 1.2 us: one_kernel(): sin_b = jnp.where(high, sin_w, 0.0)]
    slice x5 -> x0, local copies, waits for them, and re-layouts: 2.06 us -> none  [the longest x2 0.83 us: one_kernel(): qv = small[6, :3 * heads * HD].reshape(heads, 3, HD)[:, 0::2].reshape(-1)]
    pallas_call x1, Pallas kernels: 80.3 us -> 78.4 us  [one_kernel(): pl.pallas_call(functools.partial(block_kernel, tp, heads, n_copies), out_...]
    broadcast_in_dim x2 -> x0, local copies, waits for them, and re-layouts: 1.16 us -> none  [the longest x1 0.58 us: one_kernel(): upb[None]]
where the time goes in v2:
time: 81.9 us; the launch traced here: 81.7 us
  Pallas kernels  81.1 us (99%)
    pallas_call x1, Pallas kernels, one_kernel(): pl.pallas_call(functools.partial(block_kernel, tp, heads, n_copies), out_...  78.4 us
    pallas_call x1, Pallas kernels, one_kernel(): pl.pallas_call(functools.partial(settle_kernel, heads), out_shape=(sds((1...  2.69 us

profile of v2, /device:TPU:0, one launch (start us, length us, event | category | flops | bytes accessed | tf_op | source)
XLA Modules:
  0.0 81.7 jit_solution(9687911470565139076)
XLA Ops:
  0.6 78.4 %shard_map.203 = (bf16[4,64,768]{2,1,0:T(8,128)(2,1)}, bf16[4,64,768]{2,1,0:T(8,128)(2,1)}, f32[8,768]{1,0:T(8,128)}, f32[96,576]{1,0:T(8,128)}, f32[96,192]{1,0...) custom-call(bf16[4,64,768]{2,1,0:T(8,128)(2,1)} %bitcast.2, s32[1,8]{1,0:T(1,128)} %span_ref.1, f32[2,768]{1,0:T(2,128)} %gain_ref.1, ...), custom_call_target="tpu_custom_call" | custom-call | tf_op jit(solution)/shard_map/pallas_call | solution.py:745
  79.1 2.7 %shard_map.204 = (bf16[1,256,768]{2,1,0:T(8,128)(2,1)}, bf16[1,256,768]{2,1,0:T(8,128)(2,1)}, f32[2,768]{1,0:T(2,128)}, f32[2,768]{1,0:T(2,128)}, f32[96,576]{1,...) custom-call(bf16[4,64,768]{2,1,0:T(8,128)(2,1)} %get-tuple-element.1, ...), custom_call_target="tpu_custom_call" | custom-call | tf_op jit(solution)/shard_map/pallas_call | solution.py:774

commit v3 on v2

--- a/solution.py
+++ b/solution.py
@@ -497,6 +497,37 @@
     def z_gather(fin):
         return [rcopy(fin.at[z], fin.at[z], dev) for dev in z_peers]
 
+    class LineGather:
+        def __init__(self, fin):
+            self.moves = []
+            for side in (1, -1):
+                for k in range(tp - 1):
+                    src = fin.at[(z - side * k + tp) % tp]
+                    i = n_copies + len(guarded)
+                    cp = pltpu.make_async_remote_copy(
+                        src_ref=src,
+                        dst_ref=src,
+                        send_sem=ssem.at[i],
+                        recv_sem=rsem.at[i],
+                        device_id=(c, t, (z + side + tp) % tp),
+                        device_id_type=pl.DeviceIdType.MESH,
+                    )
+                    has = (z - k >= 0) if side == 1 else (z + k < tp)
+                    more = (z + 1 < tp) if side == 1 else (z >= 1)
+                    gets = (z - k - 1 >= 0) if side == 1 else (z + k + 1 < tp)
+                    guarded.append((cp, has & more))
+                    self.moves.append((k, cp, has & more, gets))
+            self.step(0)
+
+        def step(self, k):
+            for hop, cp, sends, gets in self.moves:
+                if hop == k - 1:
+                    pl.when(gets)(cp.wait_recv)
+            for hop, cp, sends, gets in self.moves:
+                if hop == k:
+                    pl.when(sends)(cp.start)
+
+    guarded = []
     ag_qkv = Gather(wqkv_ref, qkv_w)
     ag_dense = Gather(wdense_ref, dense_w)
 
@@ -619,7 +650,7 @@
     rs_qkv = Scatter(qkv_g, qkv_bufs)
     fin = z_sum(z_out, out_g, out_rcv)
     out_fin[z] = (x_ref[z].astype(F32) + outb_ref[...].reshape(1, -1) + fin).astype(BF)
-    c_out = z_gather(out_fin)
+    c_out = LineGather(out_fin)
     rs_up.first()
     rs_down.second()
     rs_dense.second()
@@ -630,10 +661,11 @@
     sm_z[z, 3:4, :] = jnp.sum(dz2, axis=0, keepdims=True)
     c_sm = z_gather(sm_z)
     rs_qkv.first()
+    c_out.step(1)
     rs_up.second()
+    me = 4 * c + t
     for cp in c_sm:
         cp.wait_recv()
-    me = 4 * c + t
     sm = sm_z[0]
     for i in range(1, tp):
         sm = sm + sm_z[i]
@@ -642,30 +674,41 @@
     sm_p[me, 5:6, 0 : dpre.shape[1]] = jnp.sum(dpre, axis=0, keepdims=True)
     sm_p[me, 6:7, 0:wide] = jnp.sum(dproj, axis=0, keepdims=True)
     c_pl = [rcopy(sm_p.at[me], sm_p.at[me], dev) for dev in peers]
+    c_out.step(2)
     tt = z_sum(z_t, t_g, t_rcv)
     xh = xhat_s[z]
     back = inv_s[z, :, 0:1] * (
         tt - jnp.mean(tt, axis=-1, keepdims=True) - xh * jnp.mean(tt * xh, axis=-1, keepdims=True)
     )
     t_fin[z] = (g_ref[z].astype(F32) + back).astype(BF)
-    c_t = z_gather(t_fin)
+    c_t = LineGather(t_fin)
     rs_qkv.second()
-    for rs, out in ((rs_dense, dense_out), (rs_down, down_out), (rs_up, up_out), (rs_qkv, qkv_out)):
+
+    def finish(rs, out):
         top, low = rs.finish()
         out[pl.ds(0, rs.h), :] = top
         out[pl.ds(rs.h, rs.h), :] = low
+
+    finish(rs_dense, dense_out)
+    finish(rs_down, down_out)
+    c_t.step(1)
+    finish(rs_up, up_out)
+    for k in range(3, tp):
+        c_out.step(k)
+    layer_out[...] = out_fin[...]
+    for k in range(2, tp - 1):
+        c_t.step(k)
+    finish(rs_qkv, qkv_out)
     for cp in c_pl:
         cp.wait_recv()
     sm = sm_p[0]
     for i in range(1, 8):
         sm = sm + sm_p[i]
     small_out[...] = sm
-    for cp in c_out:
-        cp.wait_recv()
-    layer_out[...] = out_fin[...]
-    for cp in c_t:
-        cp.wait_recv()
+    c_t.step(tp - 1)
     grad_in[...] = t_fin[...]
+    for cp, sends in guarded:
+        pl.when(sends)(cp.wait_send)
     assert len(copies) <= n_copies
     for cp in copies:
         cp.wait_send()
@@ -735,8 +778,8 @@
         vm((tok, wide), F32),
         vm((tok, wide), F32),
         vm((tok, wide), F32),
-        pltpu.SemaphoreType.DMA((n_copies,)),
-        pltpu.SemaphoreType.DMA((n_copies,)),
+        pltpu.SemaphoreType.DMA((n_copies + 4 * tp,)),
+        pltpu.SemaphoreType.DMA((n_copies + 4 * tp,)),
     ]
     vspec = pl.BlockSpec(memory_space=pltpu.VMEM)
     specs = [vspec] * 12

time: 81.9 us -> 82.5 us (level)
  no operation moved by 1% of the time
where the time goes in v3:
time: 82.5 us; the launch traced here: 82.4 us
  Pallas kernels  81.7 us (99%)
    pallas_call x1, Pallas kernels, one_kernel(): pl.pallas_call(functools.partial(block_kernel, tp, heads, n_copies), out_...  79 us
    pallas_call x1, Pallas kernels, one_kernel(): pl.pallas_call(functools.partial(settle_kernel, heads), out_shape=(sds((1...  2.69 us

profile of v3, /device:TPU:0, one launch (start us, length us, event | category | flops | bytes accessed | tf_op | source)
XLA Modules:
  0.0 82.4 jit_solution(14818978537074179367)
XLA Ops:
  0.6 79.0 %shard_map.203 = (bf16[4,64,768]{2,1,0:T(8,128)(2,1)}, bf16[4,64,768]{2,1,0:T(8,128)(2,1)}, f32[8,768]{1,0:T(8,128)}, f32[96,576]{1,0:T(8,128)}, f32[96,192]{1,0...) custom-call(bf16[4,64,768]{2,1,0:T(8,128)(2,1)} %bitcast.2, s32[1,8]{1,0:T(1,128)} %span_ref.1, f32[2,768]{1,0:T(2,128)} %gain_ref.1, ...), custom_call_target="tpu_custom_call" | custom-call | tf_op jit(solution)/shard_map/pallas_call | solution.py:788
  79.7 2.7 %shard_map.204 = (bf16[1,256,768]{2,1,0:T(8,128)(2,1)}, bf16[1,256,768]{2,1,0:T(8,128)(2,1)}, f32[2,768]{1,0:T(2,128)}, f32[2,768]{1,0:T(2,128)}, f32[96,576]{1,...) custom-call(bf16[4,64,768]{2,1,0:T(8,128)(2,1)} %get-tuple-element.1, ...), custom_call_target="tpu_custom_call" | custom-call | tf_op jit(solution)/shard_map/pallas_call | solution.py:817
